TPU v7x, 32 devices: a whole 2x2x4 slice. The times are simulated.
32 devices in a mesh: parts: 2 (over x), row: 16 (over z, y, core).
Axes of the slice: x: 2, y: 2, z: 4, core: 2. Of those that a mesh axis runs over, the one named last changes fastest.
Arguments:
- tile_values: bfloat16 [2048, 128, 128], P(('parts', 'row')), parts along dimension 0, may hold values from -0.09375 to 0.09375
- tile_row: int32 [2048], P(('parts', 'row')), parts along dimension 0, may hold values from 0 to 1
- tile_col: int32 [2048], P(('parts', 'row')), parts along dimension 0, may hold values from 0 to 15
- primal_start: float32 [4096, 128], P(('parts', 'row')), parts along dimension 0, may hold values from 0 to 1
- objective: float32 [4096, 128], P(('parts', 'row')), parts along dimension 0, may hold values from -3 to 3
- upper_bound: float32 [4096], P(('parts', 'row')), parts along dimension 0, may hold values from 0.3 to 3
- dual_start: float32 [8192, 128], P(('parts', 'row')), parts along dimension 0, may hold values from 0 to 1
- row_bound: float32 [8192, 128], P(('parts', 'row')), parts along dimension 0, may hold values from -6 to 6
Outputs:
- primal: float32 [4096, 128], P(('parts', 'row')), parts along dimension 0
- dual: float32 [8192, 128], P(('parts', 'row')), parts along dimension 0
There are 2 independent parts, one for each index of `parts`. A program takes and returns all parts, laid end to end along the dimension named above; each array names one. Nothing has to cross between parts.
All inputs are finite; a program needn't handle non-finite values.
Results may differ from a plain program's by a relative error of at most 0.0023.
Values may be sent and summed in bfloat16 or wider, within the bound.
A program may use at most 64 MiB of HBM per device.

v0:
```python
import functools

import jax
import jax.numpy as jnp
from jax import lax
from jax.experimental import pallas as pl
from jax.experimental.pallas import tpu as pltpu
from jax.sharding import PartitionSpec as P

ITERS = 3
HALVES = 2
STEP = 0.4
F32 = jnp.float32
BF16 = jnp.bfloat16


def dense_kernel(places, tiles, high, low, total):
    total[...] = jnp.zeros_like(total)

    @pl.loop(0, tiles.shape[0], unroll=8)
    def _(t):
        total[places[t]] += tiles[t].astype(F32)

    @pl.loop(0, total.shape[0], unroll=4)
    def _(b):
        value = total[b]
        rounded = value.astype(BF16)
        high[b] = rounded
        low[b] = (value - rounded.astype(F32)).astype(BF16)


def dense(tile_values, tile_row, tile_col, blocks, row_blocks):
    tiles, size, _ = tile_values.shape
    shape = jax.ShapeDtypeStruct((blocks * row_blocks, size, size), BF16)
    smem = pl.BlockSpec(memory_space=pltpu.SMEM)
    vmem = pl.BlockSpec(memory_space=pltpu.VMEM)
    room = size * size * (8 * blocks * row_blocks + 2 * tiles)
    return pl.pallas_call(
        dense_kernel,
        out_shape=(shape, shape),
        in_specs=[smem, vmem],
        out_specs=(vmem, vmem),
        scratch_shapes=[pltpu.VMEM((blocks * row_blocks, size, size), F32)],
        compiler_params=pltpu.CompilerParams(vmem_limit_bytes=room + (4 << 20)),
    )(tile_col * row_blocks + tile_row, tile_values)


def iterate_kernel(
    n, halves, high, low, primal_start, objective, upper, dual_start, row_bound,
    primal_out, dual_out,
    primal, dual, cost, bound, own, send1, recv1, send2, recv2, same, other,
    s1, r1, s2, r2, sx, rx, sf, rf,
):
    me = lax.axis_index("row")
    core = lax.rem(me, 2)
    chip = me // 2
    chips = n // 2
    partner = me + 1 - 2 * core
    size = primal.shape[1]
    part = primal.shape[0] // halves

    def peer(d):
        return lax.rem(chip + d, chips) * 2 + core

    def source(d):
        return lax.rem(chip + chips - d, chips) * 2

    def send(src, dst, send_sem, recv_sem, device):
        return pltpu.make_async_remote_copy(
            src_ref=src, dst_ref=dst, send_sem=send_sem, recv_sem=recv_sem,
            device_id={"row": device}, device_id_type=pl.DeviceIdType.MESH,
        )

    def to_partner(h, d):
        return send(send1.at[h, d], recv1.at[h, d], s1.at[h, d], r1.at[h, d], partner)

    def to_peer(h, d):
        return send(send2.at[h, d], recv2.at[h, d], s2.at[h, d], r2.at[h, d], peer(d))

    def spread(h, d):
        return send(same.at[h, 0], same.at[h, d], sx.at[h, d], rx.at[h, d], peer(d))

    def forward(h, d):
        return send(same.at[h, d], other.at[h, d], sf.at[h, d], rf.at[h, d], partner)

    order = list(range(1, chips)) + [0]

    def scenarios(h):
        return pl.ds(h * part, part)

    def wide(left, blocks, axis):
        total = None
        for ref in (high, low):
            right = jnp.concatenate([ref[c] for c in blocks], axis=1)
            value = lax.dot_general(
                left, right, (((1,), (axis,)), ((), ())), preferred_element_type=F32
            )
            total = value if total is None else total + value
        return total

    def partials(h, start):
        lowered = dual[scenarios(h), :].astype(BF16)
        for own_side in (False, True):
            for i in range(0, chips, 2):
                pair = order[i : i + 2]
                side = core if own_side else 1 - core
                value = wide(lowered, [lax.rem(chip + d, chips) * 2 + side for d in pair], 0)
                for j, d in enumerate(pair):
                    piece = value[:, j * size : (j + 1) * size]
                    if own_side:
                        own[h, d] = piece
                    else:
                        send1[h, d] = piece.astype(BF16)
                        if start:
                            to_partner(h, d).start()

    def add_partner(h):
        for d in range(1, chips):
            to_partner(h, d).wait_recv()
            send2[h, d] = (own[h, d] + recv1[h, d].astype(F32)).astype(BF16)
            to_peer(h, d).start()

    def update(h):
        to_partner(h, 0).wait_recv()
        total = own[h, 0] + recv1[h, 0].astype(F32)
        for d in range(1, chips):
            to_peer(h, d).wait_recv()
            total += recv2[h, d].astype(F32)
        before = primal[scenarios(h), :]
        updated = jnp.clip(before - STEP * (cost[scenarios(h), :] - total), 0.0, upper[...])
        same[h, 0] = (2.0 * updated - before).astype(BF16)
        for d in range(1, chips):
            spread(h, d).start()
        forward(h, 0).start()
        primal[scenarios(h), :] = updated
        for d in range(chips):
            to_partner(h, d).wait_send()

    def pass_on(h):
        for d in range(1, chips):
            spread(h, d).wait_recv()
            forward(h, d).start()
        for d in range(1, chips):
            to_peer(h, d).wait_send()

    def image(h):
        total = None
        for held, side in ((same, core), (other, 1 - core)):
            for i in range(0, chips, 2):
                pair = (i, i + 1)
                if held is other:
                    for d in pair:
                        forward(h, d).wait_recv()
                block = jnp.concatenate([held[h, d] for d in pair], axis=1)
                value = wide(block, [source(d) + side for d in pair], 1)
                total = value if total is None else total + value
        dual[scenarios(h), :] = jnp.maximum(
            dual[scenarios(h), :] + STEP * (bound[scenarios(h), :] - total), 0.0
        )
        for d in range(chips):
            forward(h, d).wait_send()
            if d:
                spread(h, d).wait_send()

    barrier = pltpu.get_barrier_semaphore()
    pl.semaphore_signal(
        barrier, inc=1, device_id={"row": partner}, device_id_type=pl.DeviceIdType.MESH
    )
    for d in range(1, chips):
        pl.semaphore_signal(
            barrier, inc=1, device_id={"row": peer(d)}, device_id_type=pl.DeviceIdType.MESH
        )
    dual[...] = dual_start[...].T
    for h in range(halves):
        partials(h, False)
    primal[...] = primal_start[...].T
    cost[...] = objective[...].T
    bound[...] = row_bound[...].T
    pl.semaphore_wait(barrier, chips)
    for h in range(halves):
        for d in order:
            to_partner(h, d).start()
    for h in range(halves):
        add_partner(h)

    def iteration(step, carry):
        more = step < ITERS - 1
        for h in range(halves):
            update(h)
        for h in range(halves):
            pass_on(h)
            if h:
                pl.when(more)(functools.partial(add_partner, h - 1))
            image(h)
            pl.when(more)(functools.partial(partials, h, True))
        pl.when(more)(functools.partial(add_partner, halves - 1))
        return carry

    lax.fori_loop(0, ITERS, iteration, 0)
    primal_out[...] = primal[...].T
    dual_out[...] = dual[...].T


def body(
    tile_values, tile_row, tile_col, primal_start, objective, upper_bound, dual_start, row_bound
):
    n = lax.axis_size("row")
    size = tile_values.shape[1]
    count = primal_start.shape[1]
    blocks = n * primal_start.shape[0] // size
    assert blocks == n and n % 4 == 0
    rows = dual_start.shape[0]
    row_blocks = rows // size
    high, low = dense(tile_values, tile_row, tile_col, blocks, row_blocks)
    chips = n // 2
    halves = HALVES
    part = count // halves
    vmem = pl.BlockSpec(memory_space=pltpu.VMEM)
    buffer = pltpu.VMEM((halves, chips, part, size), BF16)
    state = pltpu.VMEM((count, size), F32)
    long_state = pltpu.VMEM((count, rows), F32)
    room = 4 * blocks * rows * size + 16 * chips * count * size + (6 << 20)
    return pl.pallas_call(
        functools.partial(iterate_kernel, n, halves),
        out_shape=(
            jax.ShapeDtypeStruct(primal_start.shape, F32),
            jax.ShapeDtypeStruct(dual_start.shape, F32),
        ),
        in_specs=[vmem] * 7,
        out_specs=(vmem, vmem),
        scratch_shapes=[
            state, long_state, state, long_state,
            pltpu.VMEM((halves, chips, part, size), F32),
            buffer, buffer, buffer, buffer, buffer, buffer,
        ] + [pltpu.SemaphoreType.DMA((halves, chips))] * 8,
        compiler_params=pltpu.CompilerParams(
            collective_id=0, has_side_effects=True, vmem_limit_bytes=room
        ),
    )(
        high.reshape(blocks, rows, size), low.reshape(blocks, rows, size),
        primal_start, objective, upper_bound.reshape(1, -1), dual_start, row_bound,
    )


def solution(mesh):
    rows = P(("parts", "row"), None)
    flat = P(("parts", "row"))
    return jax.shard_map(
        body,
        mesh=mesh,
        in_specs=(P(("parts", "row"), None, None), flat, flat, rows, rows, flat, rows, rows),
        out_specs=(rows, rows),
        check_vma=False,
    )
```

profile of v0, /device:TPU:0, one launch (start us, length us, event | category | flops | bytes accessed | tf_op | source)
XLA Modules:
  0.0 59.0 jit_solution(6682875144262277590)
XLA Ops:
  0.6 0.0 copy-start.5
  0.6 0.7 %multiply_add_fusion.places = s32[64]{0:T(128)S(1)} fusion(s32[64]{0:T(128)} %param.9, s32[64]{0:T(128)} %param.10), kind=kLoop, calls=%fused_computation | loop fusion | flops 128 | bytes 768 | tf_op jit(solution)/shard_map/add | solution.py:45
  1.3 0.0 copy-start
  1.3 1.6 %copy-done = bf16[64,128,128]{2,1,0:T(8,128)(2,1)S(1)} copy-done((bf16[64,128,128]{2,1,0:T(8,128)(2,1)S(1)}, bf16[64,128,128]{2,1,0:T(8,128)(2,1)}, u32[]{:S(2)}) %copy-start) | copy-done | bytes 2097176
  2.9 0.0 copy-start.1
  2.9 0.0 copy-start.2
  2.9 0.0 copy-start.3
  2.9 0.0 copy-start.4
  2.9 1.4 %shard_map.95 = (bf16[32,128,128]{2,1,0:T(8,128)(2,1)S(1)}, bf16[32,128,128]{2,1,0:T(8,128)(2,1)S(1)}) custom-call(s32[64]{0:T(128)S(1)} %multiply_add_fusion.places, bf16[64,128,128]{2,1,0:T(8,128)(2,1)S(1)} %copy-done), custom_call_target="tpu_custom_call" | custom-call | tf_op jit(solution)/shard_map/pallas_call | solution.py:38
  4.3 0.0 copy-done.5
  4.3 0.0 copy-done.1
  4.3 0.0 copy-done.2
  4.3 0.0 copy-done.3
  4.3 0.0 copy-done.4
  4.4 53.4 %shard_map.96 = (f32[128,128]{1,0:T(8,128)S(1)}, f32[256,128]{1,0:T(8,128)S(1)}) custom-call(bf16[16,256,128]{2,1,0:T(8,128)(2,1)S(1)} %bitcast.3, bf16[16,256,128]{2,1,0:T(8,128)(2,1)S(1)} %bitcast.4, f32[128,128]{1,0:T(8,128)S(1)} %copy-done.3, f32[128,128]{1,0:T(8,128)S(1)} %copy-done.4, f32[1,128]{1,0:T(1,128)S(1)} %bitcast.5, f32[256,128]{1,0:T(8,128)S(1)} %copy-done.1, ...), custom_call_target="tpu_custom_call" | custom-call | tf_op jit(solution)/shard_map/pallas_call | solution.py:223
  57.7 0.6 %copy.12 = f32[128,128]{1,0:T(8,128)} copy(f32[128,128]{1,0:T(8,128)S(1)} %get-tuple-element.8) | data formatting | bytes 131072
  58.4 0.7 %copy.13 = f32[256,128]{1,0:T(8,128)} copy(f32[256,128]{1,0:T(8,128)S(1)} %get-tuple-element.9) | data formatting | bytes 262144
Async XLA Ops:
  0.6 3.7 %copy-start.5 = (f32[128]{0:T(128)S(1)}, f32[128]{0:T(128)}, u32[]{:S(2)}) copy-start(f32[128]{0:T(128)} %param.13) | copy-start | bytes 1540
  1.3 1.6 %copy-start = (bf16[64,128,128]{2,1,0:T(8,128)(2,1)S(1)}, bf16[64,128,128]{2,1,0:T(8,128)(2,1)}, u32[]{:S(2)}) copy-start(bf16[64,128,128]{2,1,0:T(8,128)(2,1)} %tiles.1) | copy-start | bytes 6291460
  2.9 1.4 %copy-start.1 = (f32[256,128]{1,0:T(8,128)S(1)}, f32[256,128]{1,0:T(8,128)}, u32[]{:S(2)}) copy-start(f32[256,128]{1,0:T(8,128)} %dual_start.1) | copy-start | bytes 393220
  2.9 1.4 %copy-start.2 = (f32[256,128]{1,0:T(8,128)S(1)}, f32[256,128]{1,0:T(8,128)}, u32[]{:S(2)}) copy-start(f32[256,128]{1,0:T(8,128)} %row_bound.1) | copy-start | bytes 393220
  2.9 1.4 %copy-start.3 = (f32[128,128]{1,0:T(8,128)S(1)}, f32[128,128]{1,0:T(8,128)}, u32[]{:S(2)}) copy-start(f32[128,128]{1,0:T(8,128)} %primal_start.1) | copy-start | bytes 196612
  2.9 1.4 %copy-start.4 = (f32[128,128]{1,0:T(8,128)S(1)}, f32[128,128]{1,0:T(8,128)}, u32[]{:S(2)}) copy-start(f32[128,128]{1,0:T(8,128)} %objective.1) | copy-start | bytes 196612
where the time goes:
time: 59.2 us; the launch traced here: 59 us
  Pallas kernels  54.8 us (93%)
  local copies, waits for them, and re-layouts  2.9 us (5%)
  between operations  0.7 us (1%)
  other arithmetic  0.68 us (1%)
    pallas_call x1, Pallas kernels, body(): pl.pallas_call(functools.partial(iterate_kernel, n, halves), out_shape=(j...  53.4 us
    unnamed x14, local copies, waits for them, and re-layouts  2.9 us
    pallas_call x1, Pallas kernels, dense(): pl.pallas_call(dense_kernel, out_shape=(shape, shape), in_specs=[smem, vm...  1.37 us

commit v1 on v0

v1 whole, which is shorter than its diff:
```python
import functools

import jax
import jax.numpy as jnp
from jax import lax
from jax.experimental import pallas as pl
from jax.experimental.pallas import tpu as pltpu
from jax.sharding import PartitionSpec as P

ITERS = 3
CHAINS = 2
STEP = 0.4
F32 = jnp.float32
BF16 = jnp.bfloat16


def dense_kernel(places, tiles, high, low, total):
    total[...] = jnp.zeros_like(total)

    @pl.loop(0, tiles.shape[0], unroll=8)
    def _(t):
        total[places[t]] += tiles[t].astype(F32)

    @pl.loop(0, total.shape[0], unroll=4)
    def _(b):
        value = total[b]
        rounded = value.astype(BF16)
        high[b] = rounded
        low[b] = (value - rounded.astype(F32)).astype(BF16)


def dense(tile_values, tile_row, tile_col, blocks, row_blocks):
    tiles, size, _ = tile_values.shape
    shape = jax.ShapeDtypeStruct((blocks * row_blocks, size, size), BF16)
    smem = pl.BlockSpec(memory_space=pltpu.SMEM)
    vmem = pl.BlockSpec(memory_space=pltpu.VMEM)
    room = size * size * (8 * blocks * row_blocks + 2 * tiles)
    return pl.pallas_call(
        dense_kernel,
        out_shape=(shape, shape),
        in_specs=[smem, vmem],
        out_specs=(vmem, vmem),
        scratch_shapes=[pltpu.VMEM((blocks * row_blocks, size, size), F32)],
        compiler_params=pltpu.CompilerParams(vmem_limit_bytes=room + (4 << 20)),
    )(tile_col * row_blocks + tile_row, tile_values)


def iterate_kernel(
    n, chains, high, low, primal_start, objective, upper, dual_start, row_bound,
    primal_out, dual_out,
    far_high, far_low, flipped, bounds, packed, state, dual, bound,
    part_own, part_send, part_recv, own, send1, recv1, half, send2, recv2, spread,
    primal_end, dual_end,
    sp, rp, sa, ra, sd, rd, si, ri, s1, r1, s2, r2, sx, rx, se, re,
):
    me = lax.axis_index("row")
    core = lax.rem(me, 2)
    chip = me // 2
    group = n // 4
    side = chip // group
    seat = lax.rem(chip, group)
    partner = me + 1 - 2 * core
    mirror = lax.rem(chip + group, 2 * group) * 2
    size = primal_start.shape[0]
    rows = dual_start.shape[0]
    mine = primal_start.shape[1] // 2
    part = mine // chains
    slot = 2 * side

    def seat_at(d):
        return lax.bitwise_xor(seat, d)

    def peer(d):
        return (side * group + seat_at(d)) * 2 + core

    def send(src, dst, send_sem, recv_sem, device):
        return pltpu.make_async_remote_copy(
            src_ref=src, dst_ref=dst, send_sem=send_sem, recv_sem=recv_sem,
            device_id={"row": device}, device_id_type=pl.DeviceIdType.MESH,
        )

    def whole(h):
        return pl.ds(h * mine, mine)

    def chain(c):
        return pl.ds(c * part, part)

    def place(c):
        return pl.ds(core * mine + c * part, part)

    def first_partial(d):
        return send(part_send.at[d], part_recv.at[d], sp.at[d], rp.at[d], partner)

    def matrix(k):
        src, dst = ((high, far_high), (low, far_low))[k]
        return send(src, dst, sa.at[k], ra.at[k], partner)

    def rows_over(k):
        src, dst = ((flipped, dual), (bounds, bound))[k]
        return send(src.at[whole(1 - core)], dst.at[1], sd.at[k], rd.at[k], partner)

    def start_state(k):
        source = packed.at[core if k == 1 else 1 - core]
        device = (partner, mirror + core, mirror + 1 - core)[k]
        return send(source, state.at[slot + core], si.at[k], ri.at[k], device)

    def reduce(c, d):
        return send(send1.at[c, d], recv1.at[c, d], s1.at[c, d], r1.at[c, d], peer(d))

    def cross(c, step):
        turn = lax.rem(step, 2)
        return send(
            send2.at[c, turn], recv2.at[c, turn], s2.at[c, turn], r2.at[c, turn], mirror + core
        )

    def gather(c, d):
        return send(spread.at[c, 0], spread.at[c, d], sx.at[c, d], rx.at[c, d], peer(d))

    def primal_back(c):
        return send(
            state.at[slot + 1 - core, chain(c)], primal_end.at[place(c)],
            se.at[0, c], re.at[0, c], partner,
        )

    def dual_back(c):
        return send(
            dual.at[1, chain(c)], dual_end.at[place(c)], se.at[1, c], re.at[1, c], partner
        )

    far_first = list(range(group - 1, 0, -1))
    near_first = list(range(1, group))

    def owned(d):
        q = seat_at(d)
        return [2 * q, 2 * q + 1, 2 * (q + group), 2 * (q + group) + 1]

    def dot(left, right, axis):
        return lax.dot_general(
            left, right, (((1,), (axis,)), ((), ())), preferred_element_type=F32
        )

    def side_by_side(ref, blocks):
        return jnp.concatenate([ref[b] for b in blocks], axis=1)

    def columns(left, blocks, pairs):
        total = None
        for refs in pairs:
            right = jnp.concatenate([side_by_side(ref, blocks) for ref in refs], axis=0)
            value = dot(left, right, 0)
            total = value if total is None else total + value
        return total

    near = ((high,), (low,))
    both = ((high, far_high), (low, far_low))

    def start():
        left = jnp.concatenate([flipped[whole(core), :], flipped[whole(1 - core), :]], axis=0)
        left = left.astype(BF16)
        for d in far_first + [0]:
            blocks = owned(d)
            for i in range(0, 4, 2):
                value = columns(left, blocks[i : i + 2], near)
                for k in range(2):
                    piece = value[:, k * size : (k + 1) * size]
                    part_own[d, i + k] = piece[:mine]
                    part_send[d, i + k] = piece[mine:].astype(BF16)

    def finish_start():
        for d in far_first + [0]:
            first_partial(d).wait_recv()
            for c in range(chains):
                value = part_own[d, :, chain(c)] + part_recv[d, :, chain(c)].astype(F32)
                if d:
                    send1[c, d] = value.astype(BF16)
                    reduce(c, d).start()
                else:
                    own[c] = value

    def partials(c):
        left = jnp.concatenate([dual[0, chain(c), :], dual[1, chain(c), :]], axis=1)
        left = left.astype(BF16)
        for d in far_first + [0]:
            blocks = owned(d)
            for i in range(0, 4, 2):
                value = columns(left, blocks[i : i + 2], both)
                for k in range(2):
                    piece = value[:, k * size : (k + 1) * size]
                    if d:
                        send1[c, d, i + k] = piece.astype(BF16)
                    else:
                        own[c, i + k] = piece
            if d:
                reduce(c, d).start()

    def merge(c, step):
        total = own[c]
        for d in near_first:
            reduce(c, d).wait_recv()
            total += recv1[c, d].astype(F32)
        half[c] = total
        send2[c, lax.rem(step, 2)] = total.astype(BF16)
        cross(c, step).start()

    def update(c, step):
        cross(c, step).wait_recv()
        total = half[c] + recv2[c, lax.rem(step, 2)].astype(F32)
        before = state[:, chain(c), :]
        cost = state[:, pl.ds(mine + c * part, part), :]
        upper_here = state[:, pl.ds(2 * mine, 1), :]
        updated = jnp.clip(before - STEP * (cost - total), 0.0, upper_here)
        spread[c, 0] = (2.0 * updated - before).astype(BF16)
        for d in far_first:
            gather(c, d).start()
        state[:, chain(c), :] = updated
        for d in near_first:
            reduce(c, d).wait_send()
        cross(c, step).wait_send()

    def image(c):
        total = None
        for d in [0] + near_first:
            if d:
                gather(c, d).wait_recv()
            blocks = owned(d)
            left = jnp.concatenate([spread[c, d, i] for i in range(4)], axis=1)
            for refs in both:
                right = jnp.concatenate([side_by_side(ref, blocks) for ref in refs], axis=0)
                value = dot(left, right, 1)
                total = value if total is None else total + value
        for k in range(2):
            dual[k, chain(c), :] = jnp.maximum(
                dual[k, chain(c), :]
                + STEP * (bound[k, chain(c), :] - total[:, k * rows : (k + 1) * rows]),
                0.0,
            )
        for d in near_first:
            gather(c, d).wait_send()

    barrier = pltpu.get_barrier_semaphore()
    others = [partner, mirror + core, mirror + 1 - core] + [peer(d) for d in near_first]
    for other in others:
        pl.semaphore_signal(
            barrier, inc=1, device_id={"row": other}, device_id_type=pl.DeviceIdType.MESH
        )
    flipped[...] = dual_start[...].T
    for source, offset in ((primal_start, 0), (objective, mine)):
        value = source[...].T
        for h in range(2):
            packed[h, pl.ds(offset, mine), :] = value[h * mine : (h + 1) * mine]
    for h in range(2):
        packed[h, pl.ds(2 * mine, 8), :] = jnp.broadcast_to(upper[...], (8, size))
    bounds[...] = row_bound[...].T
    start()
    pl.semaphore_wait(barrier, len(others))
    for d in far_first + [0]:
        first_partial(d).start()
    for k in (1, 2, 0):
        start_state(k).start()
    for k in range(2):
        rows_over(k).start()
    for k in range(2):
        matrix(k).start()
    state[slot + core] = packed[core]
    dual[0] = flipped[whole(core), :]
    bound[0] = bounds[whole(core), :]
    finish_start()
    for c in range(chains):
        merge(c, 0)
    for k in range(3):
        start_state(k).wait()
    for k in range(2):
        rows_over(k).wait()
        matrix(k).wait()
    for d in range(group):
        first_partial(d).wait_send()

    def iteration(step, carry):
        more = step < ITERS - 1
        for c in range(chains):
            update(c, step)

            @pl.when(jnp.logical_not(more))
            def _():
                primal_back(c).start()

        for c in range(chains):
            image(c)
            pl.when(more)(functools.partial(partials, c))

            @pl.when(jnp.logical_not(more))
            def _():
                dual_back(c).start()

        @pl.when(more)
        def _():
            for c in range(chains):
                merge(c, step + 1)

        return carry

    lax.fori_loop(0, ITERS, iteration, 0)
    for c in range(chains):
        primal_end[place(c), :] = state[slot + core, chain(c), :]
        dual_end[place(c), :] = dual[0, chain(c), :]
    for c in range(chains):
        primal_back(c).wait()
    primal_out[...] = primal_end[...].T
    for c in range(chains):
        dual_back(c).wait()
    dual_out[...] = dual_end[...].T


def body(
    tile_values, tile_row, tile_col, primal_start, objective, upper_bound, dual_start, row_bound
):
    n = lax.axis_size("row")
    size = tile_values.shape[1]
    count = primal_start.shape[1]
    blocks = n * primal_start.shape[0] // size
    group = n // 4
    assert blocks == n and n % 4 == 0 and group & (group - 1) == 0
    rows = dual_start.shape[0]
    row_blocks = rows // size
    high, low = dense(tile_values, tile_row, tile_col, blocks, row_blocks)
    chains = CHAINS
    mine = count // 2
    part = mine // chains
    vmem = pl.BlockSpec(memory_space=pltpu.VMEM)
    dma = pltpu.SemaphoreType.DMA
    matrix = pltpu.VMEM((blocks, rows, size), BF16)
    pieces = pltpu.VMEM((chains, group, 4, part, size), BF16)
    sums = pltpu.VMEM((chains, 4, part, size), F32)
    turns = pltpu.VMEM((chains, 2, 4, part, size), BF16)
    room = 4 * blocks * rows * size + 4 * blocks * mine * size * 8 + (8 << 20)
    return pl.pallas_call(
        functools.partial(iterate_kernel, n, chains),
        out_shape=(
            jax.ShapeDtypeStruct(primal_start.shape, F32),
            jax.ShapeDtypeStruct(dual_start.shape, F32),
        ),
        in_specs=[vmem] * 7,
        out_specs=(vmem, vmem),
        scratch_shapes=[
            matrix, matrix,
            pltpu.VMEM((count, rows), F32), pltpu.VMEM((count, rows), F32),
            pltpu.VMEM((2, count + 8, size), F32), pltpu.VMEM((4, count + 8, size), F32),
            pltpu.VMEM((2, mine, rows), F32), pltpu.VMEM((2, mine, rows), F32),
            pltpu.VMEM((group, 4, mine, size), F32),
            pltpu.VMEM((group, 4, mine, size), BF16), pltpu.VMEM((group, 4, mine, size), BF16),
            sums, pieces, pieces, sums, turns, turns, pieces,
            pltpu.VMEM((count, size), F32), pltpu.VMEM((count, rows), F32),
        ]
        + [dma((group,))] * 2 + [dma((2,))] * 4 + [dma((3,))] * 2
        + [dma((chains, group))] * 2 + [dma((chains, 2))] * 2 + [dma((chains, group))] * 2
        + [dma((2, chains))] * 2,
        compiler_params=pltpu.CompilerParams(
            collective_id=0, has_side_effects=True, vmem_limit_bytes=room
        ),
    )(
        high.reshape(blocks, rows, size), low.reshape(blocks, rows, size),
        primal_start, objective, upper_bound.reshape(1, -1), dual_start, row_bound,
    )


def solution(mesh):
    rows = P(("parts", "row"), None)
    flat = P(("parts", "row"))
    return jax.shard_map(
        body,
        mesh=mesh,
        in_specs=(P(("parts", "row"), None, None), flat, flat, rows, rows, flat, rows, rows),
        out_specs=(rows, rows),
        check_vma=False,
    )
```

time: 59.2 us -> 54.9 us (0.927)
  Pallas kernels: 54.8 us -> 50.5 us
    pallas_call x1, Pallas kernels: 53.4 us -> 49.1 us  [body(): pl.pallas_call(functools.partial(iterate_kernel, n, chains), out_shape=(j...]
where the time goes in v1:
time: 54.9 us; the launch traced here: 54.8 us
  Pallas kernels  50.5 us (92%)
  local copies, waits for them, and re-layouts  2.9 us (5%)
  between operations  0.7 us (1%)
  other arithmetic  0.68 us (1%)
    pallas_call x1, Pallas kernels, body(): pl.pallas_call(functools.partial(iterate_kernel, n, chains), out_shape=(j...  49.1 us
    unnamed x14, local copies, waits for them, and re-layouts  2.9 us
    pallas_call x1, Pallas kernels, dense(): pl.pallas_call(dense_kernel, out_shape=(shape, shape), in_specs=[smem, vm...  1.37 us

profile of v1, /device:TPU:0, one launch (start us, length us, event | category | flops | bytes accessed | tf_op | source)
XLA Modules:
  0.0 54.8 jit_solution(15627661788775358102)
XLA Ops:
  0.6 0.0 copy-start.5
  0.6 0.7 %multiply_add_fusion.places = s32[64]{0:T(128)S(1)} fusion(s32[64]{0:T(128)} %param.9, s32[64]{0:T(128)} %param.10), kind=kLoop, calls=%fused_computation | loop fusion | flops 128 | bytes 768 | tf_op jit(solution)/shard_map/add | solution.py:45
  1.3 0.0 copy-start
  1.3 1.6 %copy-done = bf16[64,128,128]{2,1,0:T(8,128)(2,1)S(1)} copy-done((bf16[64,128,128]{2,1,0:T(8,128)(2,1)S(1)}, bf16[64,128,128]{2,1,0:T(8,128)(2,1)}, u32[]{:S(2)}) %copy-start) | copy-done | bytes 2097176
  2.9 0.0 copy-start.1
  2.9 0.0 copy-start.2
  2.9 0.0 copy-start.3
  2.9 0.0 copy-start.4
  2.9 1.4 %shard_map.95 = (bf16[32,128,128]{2,1,0:T(8,128)(2,1)S(1)}, bf16[32,128,128]{2,1,0:T(8,128)(2,1)S(1)}) custom-call(s32[64]{0:T(128)S(1)} %multiply_add_fusion.places, bf16[64,128,128]{2,1,0:T(8,128)(2,1)S(1)} %copy-done), custom_call_target="tpu_custom_call" | custom-call | tf_op jit(solution)/shard_map/pallas_call | solution.py:38
  4.3 0.0 copy-done.5
  4.3 0.0 copy-done.1
  4.3 0.0 copy-done.2
  4.3 0.0 copy-done.3
  4.3 0.0 copy-done.4
  4.4 49.1 %shard_map.96 = (f32[128,128]{1,0:T(8,128)S(1)}, f32[256,128]{1,0:T(8,128)S(1)}) custom-call(bf16[16,256,128]{2,1,0:T(8,128)(2,1)S(1)} %bitcast.3, bf16[16,256,128]{2,1,0:T(8,128)(2,1)S(1)} %bitcast.4, f32[128,128]{1,0:T(8,128)S(1)} %copy-done.3, f32[128,128]{1,0:T(8,128)S(1)} %copy-done.4, f32[1,128]{1,0:T(1,128)S(1)} %bitcast.5, f32[256,128]{1,0:T(8,128)S(1)} %copy-done.1, ...), custom_call_target="tpu_custom_call" | custom-call | tf_op jit(solution)/shard_map/pallas_call | solution.py:335
  53.5 0.6 %copy.12 = f32[128,128]{1,0:T(8,128)} copy(f32[128,128]{1,0:T(8,128)S(1)} %get-tuple-element.8) | data formatting | bytes 131072
  54.1 0.7 %copy.13 = f32[256,128]{1,0:T(8,128)} copy(f32[256,128]{1,0:T(8,128)S(1)} %get-tuple-element.9) | data formatting | bytes 262144
Async XLA Ops:
  0.6 3.7 %copy-start.5 = (f32[128]{0:T(128)S(1)}, f32[128]{0:T(128)}, u32[]{:S(2)}) copy-start(f32[128]{0:T(128)} %param.13) | copy-start | bytes 1540
  1.3 1.6 %copy-start = (bf16[64,128,128]{2,1,0:T(8,128)(2,1)S(1)}, bf16[64,128,128]{2,1,0:T(8,128)(2,1)}, u32[]{:S(2)}) copy-start(bf16[64,128,128]{2,1,0:T(8,128)(2,1)} %tiles.1) | copy-start | bytes 6291460
  2.9 1.4 %copy-start.1 = (f32[256,128]{1,0:T(8,128)S(1)}, f32[256,128]{1,0:T(8,128)}, u32[]{:S(2)}) copy-start(f32[256,128]{1,0:T(8,128)} %dual_start.1) | copy-start | bytes 393220
  2.9 1.4 %copy-start.2 = (f32[256,128]{1,0:T(8,128)S(1)}, f32[256,128]{1,0:T(8,128)}, u32[]{:S(2)}) copy-start(f32[256,128]{1,0:T(8,128)} %row_bound.1) | copy-start | bytes 393220
  2.9 1.4 %copy-start.3 = (f32[128,128]{1,0:T(8,128)S(1)}, f32[128,128]{1,0:T(8,128)}, u32[]{:S(2)}) copy-start(f32[128,128]{1,0:T(8,128)} %primal_start.1) | copy-start | bytes 196612
  2.9 1.4 %copy-start.4 = (f32[128,128]{1,0:T(8,128)S(1)}, f32[128,128]{1,0:T(8,128)}, u32[]{:S(2)}) copy-start(f32[128,128]{1,0:T(8,128)} %objective.1) | copy-start | bytes 196612

commit v2 on v1

--- a/solution.py
+++ b/solution.py
@@ -14,44 +14,60 @@
 BF16 = jnp.bfloat16
 
 
-def dense_kernel(places, tiles, high, low, total):
-    total[...] = jnp.zeros_like(total)
-
-    @pl.loop(0, tiles.shape[0], unroll=8)
-    def _(t):
-        total[places[t]] += tiles[t].astype(F32)
-
-    @pl.loop(0, total.shape[0], unroll=4)
-    def _(b):
-        value = total[b]
-        rounded = value.astype(BF16)
-        high[b] = rounded
-        low[b] = (value - rounded.astype(F32)).astype(BF16)
-
-
-def dense(tile_values, tile_row, tile_col, blocks, row_blocks):
-    tiles, size, _ = tile_values.shape
-    shape = jax.ShapeDtypeStruct((blocks * row_blocks, size, size), BF16)
-    smem = pl.BlockSpec(memory_space=pltpu.SMEM)
-    vmem = pl.BlockSpec(memory_space=pltpu.VMEM)
-    room = size * size * (8 * blocks * row_blocks + 2 * tiles)
-    return pl.pallas_call(
-        dense_kernel,
-        out_shape=(shape, shape),
-        in_specs=[smem, vmem],
-        out_specs=(vmem, vmem),
-        scratch_shapes=[pltpu.VMEM((blocks * row_blocks, size, size), F32)],
-        compiler_params=pltpu.CompilerParams(vmem_limit_bytes=room + (4 << 20)),
-    )(tile_col * row_blocks + tile_row, tile_values)
+def finish_kernel(primal, dual, primal_out, dual_out):
+    primal_out[...] = primal[...].T
+    dual_out[...] = dual[...].T
+
+
+def order_tiles(tile_row, tile_col, table, row_blocks):
+    tiles = tile_row.shape[1]
+    lanes = table.shape[1]
+    across = tile_col[...] * row_blocks + tile_row[...]
+    s = lax.broadcasted_iota(jnp.int32, (tiles, tiles), 0)
+    t = lax.broadcasted_iota(jnp.int32, (tiles, tiles), 1)
+    across = jnp.broadcast_to(across, (tiles, tiles))
+    down = jnp.sum(jnp.where(s == t, across, 0), axis=1, keepdims=True)
+    before = jnp.logical_or(across < down, jnp.logical_and(across == down, t < s))
+    rank = jnp.sum(before.astype(jnp.int32), axis=1, keepdims=True)
+    lane = lax.broadcasted_iota(jnp.int32, (tiles, lanes), 1)
+    index = lax.broadcasted_iota(jnp.int32, (tiles, lanes), 0)
+    here = rank == lane
+    table[0:1, :] = jnp.sum(jnp.where(here, index, 0), axis=0, keepdims=True)
+    table[1:2, :] = jnp.sum(jnp.where(here, down, 0), axis=0, keepdims=True)
+    below = jnp.sum((down <= lane).astype(jnp.int32), axis=0, keepdims=True)
+    equal = jnp.sum((down == lane).astype(jnp.int32), axis=0, keepdims=True)
+    table[2:3, :] = jnp.where(equal > 0, below - 1, tiles)
+
+
+def sum_tiles(tiles, order, sums, high, low):
+    count, size, _ = tiles.shape
+    row_blocks = high.shape[1] // size
+    sums[count] = jnp.zeros((size, size), F32)
+
+    def add(r, total):
+        again = order[1, r] == order[1, jnp.maximum(r - 1, 0)]
+        total = jnp.where(again, total, 0.0) + tiles[order[0, r]].astype(F32)
+        sums[r] = total
+        return total
+
+    lax.fori_loop(0, count, add, jnp.zeros((size, size), F32), unroll=4)
+
+    @pl.loop(0, high.shape[0], unroll=2)
+    def _(c):
+        for k in range(row_blocks):
+            value = sums[order[2, c * row_blocks + k]]
+            rounded = value.astype(BF16)
+            high[c, k * size : (k + 1) * size] = rounded
+            low[c, k * size : (k + 1) * size] = (value - rounded.astype(F32)).astype(BF16)
 
 
 def iterate_kernel(
-    n, chains, high, low, primal_start, objective, upper, dual_start, row_bound,
-    primal_out, dual_out,
-    far_high, far_low, flipped, bounds, packed, state, dual, bound,
+    n, chains, tiles_in, tile_row_in, tile_col_in, primal_in, objective_in, upper_in, dual_in,
+    bound_in, primal_end, dual_end,
+    tiles, tile_row, tile_col, primal_start, objective, upper, dual_start, row_bound,
+    table, order, summed, high, low, far_high, far_low, flipped, bounds, packed, state, dual, bound,
     part_own, part_send, part_recv, own, send1, recv1, half, send2, recv2, spread,
-    primal_end, dual_end,
-    sp, rp, sa, ra, sd, rd, si, ri, s1, r1, s2, r2, sx, rx, se, re,
+    sl, st, sp, rp, sa, ra, sd, rd, si, ri, s1, r1, s2, r2, sx, rx, se, re,
 ):
     me = lax.axis_index("row")
     core = lax.rem(me, 2)
@@ -61,9 +77,9 @@
     seat = lax.rem(chip, group)
     partner = me + 1 - 2 * core
     mirror = lax.rem(chip + group, 2 * group) * 2
-    size = primal_start.shape[0]
-    rows = dual_start.shape[0]
-    mine = primal_start.shape[1] // 2
+    size = primal_in.shape[0]
+    rows = dual_in.shape[0]
+    mine = primal_in.shape[1] // 2
     part = mine // chains
     slot = 2 * side
 
@@ -88,8 +104,18 @@
     def place(c):
         return pl.ds(core * mine + c * part, part)
 
-    def first_partial(d):
-        return send(part_send.at[d], part_recv.at[d], sp.at[d], rp.at[d], partner)
+    def load(k):
+        src, dst = (
+            (tile_col_in, tile_col), (tile_row_in, tile_row), (dual_in, dual_start),
+            (tiles_in, tiles), (primal_in, primal_start), (objective_in, objective),
+            (upper_in, upper), (bound_in, row_bound),
+        )[k]
+        return pltpu.make_async_copy(src, dst, sl.at[k])
+
+    def first_partial(c, d):
+        return send(
+            part_send.at[c, d], part_recv.at[c, d], sp.at[c, d], rp.at[c, d], partner
+        )
 
     def matrix(k):
         src, dst = ((high, far_high), (low, far_low))[k]
@@ -162,14 +188,16 @@
                 value = columns(left, blocks[i : i + 2], near)
                 for k in range(2):
                     piece = value[:, k * size : (k + 1) * size]
-                    part_own[d, i + k] = piece[:mine]
-                    part_send[d, i + k] = piece[mine:].astype(BF16)
+                    for c in range(chains):
+                        at = c * part
+                        part_own[c, d, i + k] = piece[at : at + part]
+                        part_send[c, d, i + k] = piece[mine + at : mine + at + part].astype(BF16)
 
     def finish_start():
-        for d in far_first + [0]:
-            first_partial(d).wait_recv()
-            for c in range(chains):
-                value = part_own[d, :, chain(c)] + part_recv[d, :, chain(c)].astype(F32)
+        for c in range(chains):
+            for d in far_first + [0]:
+                first_partial(c, d).wait_recv()
+                value = part_own[c, d] + part_recv[c, d].astype(F32)
                 if d:
                     send1[c, d] = value.astype(BF16)
                     reduce(c, d).start()
@@ -242,7 +270,21 @@
         pl.semaphore_signal(
             barrier, inc=1, device_id={"row": other}, device_id_type=pl.DeviceIdType.MESH
         )
+    for k in range(8):
+        load(k).start()
+    load(0).wait()
+    load(1).wait()
+    order_tiles(tile_row, tile_col, table, rows // size)
+    to_scalars = pltpu.make_async_copy(table, order, st)
+    to_scalars.start()
+    load(2).wait()
     flipped[...] = dual_start[...].T
+    to_scalars.wait()
+    load(3).wait()
+    sum_tiles(tiles, order, summed, high, low)
+    start()
+    for k in range(4, 8):
+        load(k).wait()
     for source, offset in ((primal_start, 0), (objective, mine)):
         value = source[...].T
         for h in range(2):
@@ -250,10 +292,10 @@
     for h in range(2):
         packed[h, pl.ds(2 * mine, 8), :] = jnp.broadcast_to(upper[...], (8, size))
     bounds[...] = row_bound[...].T
-    start()
     pl.semaphore_wait(barrier, len(others))
-    for d in far_first + [0]:
-        first_partial(d).start()
+    for c in range(chains):
+        for d in far_first + [0]:
+            first_partial(c, d).start()
     for k in (1, 2, 0):
         start_state(k).start()
     for k in range(2):
@@ -271,8 +313,9 @@
     for k in range(2):
         rows_over(k).wait()
         matrix(k).wait()
-    for d in range(group):
-        first_partial(d).wait_send()
+    for c in range(chains):
+        for d in range(group):
+            first_partial(c, d).wait_send()
 
     def iteration(step, carry):
         more = step < ITERS - 1
@@ -304,10 +347,7 @@
         dual_end[place(c), :] = dual[0, chain(c), :]
     for c in range(chains):
         primal_back(c).wait()
-    primal_out[...] = primal_end[...].T
-    for c in range(chains):
         dual_back(c).wait()
-    dual_out[...] = dual_end[...].T
 
 
 def body(
@@ -321,45 +361,63 @@
     assert blocks == n and n % 4 == 0 and group & (group - 1) == 0
     rows = dual_start.shape[0]
     row_blocks = rows // size
-    high, low = dense(tile_values, tile_row, tile_col, blocks, row_blocks)
+    tiles = tile_values.shape[0]
     chains = CHAINS
     mine = count // 2
     part = mine // chains
+    lanes = -(-max(tiles, blocks * row_blocks) // 128) * 128
     vmem = pl.BlockSpec(memory_space=pltpu.VMEM)
     dma = pltpu.SemaphoreType.DMA
     matrix = pltpu.VMEM((blocks, rows, size), BF16)
+    column = pltpu.VMEM(primal_start.shape, F32)
+    row = pltpu.VMEM(dual_start.shape, F32)
     pieces = pltpu.VMEM((chains, group, 4, part, size), BF16)
     sums = pltpu.VMEM((chains, 4, part, size), F32)
     turns = pltpu.VMEM((chains, 2, 4, part, size), BF16)
-    room = 4 * blocks * rows * size + 4 * blocks * mine * size * 8 + (8 << 20)
-    return pl.pallas_call(
+    room = (
+        8 * blocks * rows * size + 6 * (tiles + 1) * size * size
+        + 32 * blocks * mine * size + (8 << 20)
+    )
+    primal_end, dual_end = pl.pallas_call(
         functools.partial(iterate_kernel, n, chains),
         out_shape=(
-            jax.ShapeDtypeStruct(primal_start.shape, F32),
-            jax.ShapeDtypeStruct(dual_start.shape, F32),
+            jax.ShapeDtypeStruct((count, size), F32), jax.ShapeDtypeStruct((count, rows), F32)
         ),
-        in_specs=[vmem] * 7,
+        in_specs=[pl.BlockSpec(memory_space=pltpu.HBM)] * 8,
         out_specs=(vmem, vmem),
         scratch_shapes=[
-            matrix, matrix,
+            pltpu.VMEM(tile_values.shape, BF16),
+            pltpu.VMEM((1, tiles), jnp.int32), pltpu.VMEM((1, tiles), jnp.int32),
+            column, column, pltpu.VMEM((1, size), F32), row, row,
+            pltpu.VMEM((8, lanes), jnp.int32), pltpu.SMEM((8, lanes), jnp.int32),
+            pltpu.VMEM((tiles + 1, size, size), F32),
+            matrix, matrix, matrix, matrix,
             pltpu.VMEM((count, rows), F32), pltpu.VMEM((count, rows), F32),
             pltpu.VMEM((2, count + 8, size), F32), pltpu.VMEM((4, count + 8, size), F32),
             pltpu.VMEM((2, mine, rows), F32), pltpu.VMEM((2, mine, rows), F32),
-            pltpu.VMEM((group, 4, mine, size), F32),
-            pltpu.VMEM((group, 4, mine, size), BF16), pltpu.VMEM((group, 4, mine, size), BF16),
+            pltpu.VMEM((chains, group, 4, part, size), F32), pieces, pieces,
             sums, pieces, pieces, sums, turns, turns, pieces,
-            pltpu.VMEM((count, size), F32), pltpu.VMEM((count, rows), F32),
+            dma((8,)), dma(()),
         ]
-        + [dma((group,))] * 2 + [dma((2,))] * 4 + [dma((3,))] * 2
+        + [dma((chains, group))] * 2 + [dma((2,))] * 4 + [dma((3,))] * 2
         + [dma((chains, group))] * 2 + [dma((chains, 2))] * 2 + [dma((chains, group))] * 2
         + [dma((2, chains))] * 2,
         compiler_params=pltpu.CompilerParams(
             collective_id=0, has_side_effects=True, vmem_limit_bytes=room
         ),
     )(
-        high.reshape(blocks, rows, size), low.reshape(blocks, rows, size),
-        primal_start, objective, upper_bound.reshape(1, -1), dual_start, row_bound,
+        tile_values, tile_row.reshape(1, -1), tile_col.reshape(1, -1), primal_start, objective,
+        upper_bound.reshape(1, -1), dual_start, row_bound,
     )
+    return pl.pallas_call(
+        finish_kernel,
+        out_shape=(
+            jax.ShapeDtypeStruct(primal_start.shape, F32),
+            jax.ShapeDtypeStruct(dual_start.shape, F32),
+        ),
+        in_specs=[vmem] * 2,
+        out_specs=(vmem, vmem),
+    )(primal_end, dual_end)
 
 
 def solution(mesh):

time: 54.9 us -> 60.6 us (1.10)
  local copies, waits for them, and re-layouts: 2.9 us -> 8.3 us
  Pallas kernels: 50.5 us -> 51.3 us
  other arithmetic: 0.68 us -> 0 us
    unnamed x14 -> x20, local copies, waits for them, and re-layouts: 2.9 us -> 8.3 us
    add x1 -> x0, other arithmetic: 0.68 us -> none  [dense(): tile_col * row_blocks + tile_row]
where the time goes in v2:
time: 60.6 us; the launch traced here: 60.2 us
  Pallas kernels  51.3 us (85%)
  local copies, waits for them, and re-layouts  8.3 us (14%)
  between operations  0.67 us (1%)
    pallas_call x1, Pallas kernels, body(): pl.pallas_call(functools.partial(iterate_kernel, n, chains), out_shape=(j...  49.5 us
    unnamed x20, local copies, waits for them, and re-layouts  8.3 us
    pallas_call x1, Pallas kernels, body(): pl.pallas_call(finish_kernel, out_shape=(jax.ShapeDtypeStruct(primal_star...  1.73 us

profile of v2, /device:TPU:0, one launch (start us, length us, event | category | flops | bytes accessed | tf_op | source)
XLA Modules:
  0.0 60.2 jit_solution(3127080532325741278)
XLA Ops:
  0.6 0.0 copy-start
  0.6 1.6 %copy-done = bf16[64,128,128]{2,1,0:T(8,128)(2,1)S(1)} copy-done((bf16[64,128,128]{2,1,0:T(8,128)(2,1)S(1)}, bf16[64,128,128]{2,1,0:T(8,128)(2,1)}, u32[]{:S(2)}) %copy-start) | copy-done | bytes 2097176
  2.2 0.0 copy-start.1
  2.2 0.9 %copy-done.1 = f32[256,128]{1,0:T(8,128)S(1)} copy-done((f32[256,128]{1,0:T(8,128)S(1)}, f32[256,128]{1,0:T(8,128)}, u32[]{:S(2)}) %copy-start.1) | copy-done | bytes 131096
  3.1 0.0 copy-start.2
  3.1 0.9 %copy-done.2 = f32[256,128]{1,0:T(8,128)S(1)} copy-done((f32[256,128]{1,0:T(8,128)S(1)}, f32[256,128]{1,0:T(8,128)}, u32[]{:S(2)}) %copy-start.2) | copy-done | bytes 131096
  4.0 0.0 copy-start.4
  4.0 0.8 %copy-done.4 = f32[128,128]{1,0:T(8,128)S(1)} copy-done((f32[128,128]{1,0:T(8,128)S(1)}, f32[128,128]{1,0:T(8,128)}, u32[]{:S(2)}) %copy-start.4) | copy-done | bytes 65560
  4.9 0.0 copy-start.5
  4.9 0.8 %copy-done.5 = f32[128,128]{1,0:T(8,128)S(1)} copy-done((f32[128,128]{1,0:T(8,128)S(1)}, f32[128,128]{1,0:T(8,128)}, u32[]{:S(2)}) %copy-start.5) | copy-done | bytes 65560
  5.7 0.0 copy-start.7
  5.7 0.7 %copy-done.7 = s32[64]{0:T(128)S(1)} copy-done((s32[64]{0:T(128)S(1)}, s32[64]{0:T(128)}, u32[]{:S(2)}) %copy-start.7) | copy-done | bytes 280
  6.4 0.0 copy-start.8
  6.4 0.7 %copy-done.8 = s32[64]{0:T(128)S(1)} copy-done((s32[64]{0:T(128)S(1)}, s32[64]{0:T(128)}, u32[]{:S(2)}) %copy-start.8) | copy-done | bytes 280
  7.0 0.0 copy-start.9
  7.0 0.7 %copy-done.9 = f32[128]{0:T(128)S(1)} copy-done((f32[128]{0:T(128)S(1)}, f32[128]{0:T(128)}, u32[]{:S(2)}) %copy-start.9) | copy-done | bytes 536
  7.7 49.5 %shard_map.95 = (f32[128,128]{1,0:T(8,128)S(1)}, f32[128,256]{1,0:T(8,128)S(1)}) custom-call(bf16[64,128,128]{2,1,0:T(8,128)(2,1)S(1)} %copy-done, s32[1,64]{1,0:T(1,128)S(1)} %bitcast.3, s32[1,64]{1,0:T(1,128)S(1)} %bitcast.4, f32[128,128]{1,0:T(8,128)S(1)} %copy-done.4, f32[128,128]{1,0:T(8,128)S(1)} %copy-done.5, f32[1,128]{1,0:T(1,128)S(1)} %bitcast.5, ...), custom_call_target="tpu_custom_call" | custom-call | tf_op jit(solution)/shard_map/pallas_call | solution.py:381
  57.2 0.0 copy-start.3
  57.2 0.6 %copy-done.3 = f32[128,256]{1,0:T(8,128)} copy-done((f32[128,256]{1,0:T(8,128)}, f32[128,256]{1,0:T(8,128)S(1)}, u32[]{:S(2)}) %copy-start.3) | copy-done | bytes 131096
  57.9 0.0 copy-start.6
  57.9 0.6 %copy-done.6 = f32[128,128]{1,0:T(8,128)} copy-done((f32[128,128]{1,0:T(8,128)}, f32[128,128]{1,0:T(8,128)S(1)}, u32[]{:S(2)}) %copy-start.6) | copy-done | bytes 65560
  58.5 1.7 %shard_map.96 = (f32[128,128]{1,0:T(8,128)}, f32[256,128]{1,0:T(8,128)}) custom-call(f32[128,128]{1,0:T(8,128)} %copy-done.6, f32[128,256]{1,0:T(8,128)} %copy-done.3), custom_call_target="tpu_custom_call" | custom-call | tf_op jit(solution)/shard_map/pallas_call | solution.py:412
Async XLA Ops:
  0.6 1.6 %copy-start = (bf16[64,128,128]{2,1,0:T(8,128)(2,1)S(1)}, bf16[64,128,128]{2,1,0:T(8,128)(2,1)}, u32[]{:S(2)}) copy-start(bf16[64,128,128]{2,1,0:T(8,128)(2,1)} %tiles_in.1) | copy-start | bytes 6291460
  2.2 0.9 %copy-start.1 = (f32[256,128]{1,0:T(8,128)S(1)}, f32[256,128]{1,0:T(8,128)}, u32[]{:S(2)}) copy-start(f32[256,128]{1,0:T(8,128)} %dual_in.1) | copy-start | bytes 393220
  3.1 0.9 %copy-start.2 = (f32[256,128]{1,0:T(8,128)S(1)}, f32[256,128]{1,0:T(8,128)}, u32[]{:S(2)}) copy-start(f32[256,128]{1,0:T(8,128)} %bound_in.1) | copy-start | bytes 393220
  4.0 0.8 %copy-start.4 = (f32[128,128]{1,0:T(8,128)S(1)}, f32[128,128]{1,0:T(8,128)}, u32[]{:S(2)}) copy-start(f32[128,128]{1,0:T(8,128)} %primal_in.1) | copy-start | bytes 196612
  4.9 0.8 %copy-start.5 = (f32[128,128]{1,0:T(8,128)S(1)}, f32[128,128]{1,0:T(8,128)}, u32[]{:S(2)}) copy-start(f32[128,128]{1,0:T(8,128)} %objective_in.1) | copy-start | bytes 196612
  5.7 0.7 %copy-start.7 = (s32[64]{0:T(128)S(1)}, s32[64]{0:T(128)}, u32[]{:S(2)}) copy-start(s32[64]{0:T(128)} %param.9) | copy-start | bytes 772
  6.4 0.7 %copy-start.8 = (s32[64]{0:T(128)S(1)}, s32[64]{0:T(128)}, u32[]{:S(2)}) copy-start(s32[64]{0:T(128)} %param.10) | copy-start | bytes 772
  7.0 0.7 %copy-start.9 = (f32[128]{0:T(128)S(1)}, f32[128]{0:T(128)}, u32[]{:S(2)}) copy-start(f32[128]{0:T(128)} %param.13) | copy-start | bytes 1540
  57.2 0.6 %copy-start.3 = (f32[128,256]{1,0:T(8,128)}, f32[128,256]{1,0:T(8,128)S(1)}, u32[]{:S(2)}) copy-start(f32[128,256]{1,0:T(8,128)S(1)} %get-tuple-element.5.dual) | copy-start | bytes 393220
  57.9 0.6 %copy-start.6 = (f32[128,128]{1,0:T(8,128)}, f32[128,128]{1,0:T(8,128)S(1)}, u32[]{:S(2)}) copy-start(f32[128,128]{1,0:T(8,128)S(1)} %get-tuple-element.4.primal) | copy-start | bytes 196612

commit v3 on v2

--- a/solution.py
+++ b/solution.py
@@ -65,29 +65,26 @@
     n, chains, tiles_in, tile_row_in, tile_col_in, primal_in, objective_in, upper_in, dual_in,
     bound_in, primal_end, dual_end,
     tiles, tile_row, tile_col, primal_start, objective, upper, dual_start, row_bound,
-    table, order, summed, high, low, far_high, far_low, flipped, bounds, packed, state, dual, bound,
-    part_own, part_send, part_recv, own, send1, recv1, half, send2, recv2, spread,
-    sl, st, sp, rp, sa, ra, sd, rd, si, ri, s1, r1, s2, r2, sx, rx, se, re,
+    table, order, summed, high, low, far_high, far_low, high_turned, low_turned,
+    flipped, bounds, packed, state, dual, bound,
+    part_own, part_send, part_recv, own, send1, recv1, spread,
+    sl, st, sp, rp, sa, ra, sd, rd, si, ri, s1, r1, sx, rx, se, re,
 ):
     me = lax.axis_index("row")
     core = lax.rem(me, 2)
     chip = me // 2
-    group = n // 4
-    side = chip // group
-    seat = lax.rem(chip, group)
+    chips = n // 2
     partner = me + 1 - 2 * core
-    mirror = lax.rem(chip + group, 2 * group) * 2
     size = primal_in.shape[0]
     rows = dual_in.shape[0]
     mine = primal_in.shape[1] // 2
     part = mine // chains
-    slot = 2 * side
-
-    def seat_at(d):
-        return lax.bitwise_xor(seat, d)
+
+    def chip_at(d):
+        return lax.bitwise_xor(chip, d)
 
     def peer(d):
-        return (side * group + seat_at(d)) * 2 + core
+        return chip_at(d) * 2 + core
 
     def send(src, dst, send_sem, recv_sem, device):
         return pltpu.make_async_remote_copy(
@@ -125,27 +122,18 @@
         src, dst = ((flipped, dual), (bounds, bound))[k]
         return send(src.at[whole(1 - core)], dst.at[1], sd.at[k], rd.at[k], partner)
 
-    def start_state(k):
-        source = packed.at[core if k == 1 else 1 - core]
-        device = (partner, mirror + core, mirror + 1 - core)[k]
-        return send(source, state.at[slot + core], si.at[k], ri.at[k], device)
+    def start_state():
+        return send(packed.at[1 - core], state.at[core], si, ri, partner)
 
     def reduce(c, d):
         return send(send1.at[c, d], recv1.at[c, d], s1.at[c, d], r1.at[c, d], peer(d))
 
-    def cross(c, step):
-        turn = lax.rem(step, 2)
-        return send(
-            send2.at[c, turn], recv2.at[c, turn], s2.at[c, turn], r2.at[c, turn], mirror + core
-        )
-
     def gather(c, d):
         return send(spread.at[c, 0], spread.at[c, d], sx.at[c, d], rx.at[c, d], peer(d))
 
     def primal_back(c):
         return send(
-            state.at[slot + 1 - core, chain(c)], primal_end.at[place(c)],
-            se.at[0, c], re.at[0, c], partner,
+            state.at[1 - core, chain(c)], primal_end.at[place(c)], se.at[0, c], re.at[0, c], partner
         )
 
     def dual_back(c):
@@ -153,45 +141,34 @@
             dual.at[1, chain(c)], dual_end.at[place(c)], se.at[1, c], re.at[1, c], partner
         )
 
-    far_first = list(range(group - 1, 0, -1))
-    near_first = list(range(1, group))
-
-    def owned(d):
-        q = seat_at(d)
-        return [2 * q, 2 * q + 1, 2 * (q + group), 2 * (q + group) + 1]
-
-    def dot(left, right, axis):
+    far_first = list(range(chips - 1, 0, -1))
+    near_first = list(range(1, chips))
+
+    def dot(left, right):
         return lax.dot_general(
-            left, right, (((1,), (axis,)), ((), ())), preferred_element_type=F32
-        )
-
-    def side_by_side(ref, blocks):
-        return jnp.concatenate([ref[b] for b in blocks], axis=1)
-
-    def columns(left, blocks, pairs):
+            left, right, (((1,), (0,)), ((), ())), preferred_element_type=F32
+        )
+
+    def columns(left, d, pairs):
+        q = 2 * chip_at(d)
         total = None
         for refs in pairs:
-            right = jnp.concatenate([side_by_side(ref, blocks) for ref in refs], axis=0)
-            value = dot(left, right, 0)
+            right = jnp.concatenate(
+                [jnp.concatenate([ref[q], ref[q + 1]], axis=1) for ref in refs], axis=0
+            )
+            value = dot(left, right)
             total = value if total is None else total + value
-        return total
-
-    near = ((high,), (low,))
-    both = ((high, far_high), (low, far_low))
+        return [total[:, k * size : (k + 1) * size] for k in range(2)]
 
     def start():
         left = jnp.concatenate([flipped[whole(core), :], flipped[whole(1 - core), :]], axis=0)
         left = left.astype(BF16)
         for d in far_first + [0]:
-            blocks = owned(d)
-            for i in range(0, 4, 2):
-                value = columns(left, blocks[i : i + 2], near)
-                for k in range(2):
-                    piece = value[:, k * size : (k + 1) * size]
-                    for c in range(chains):
-                        at = c * part
-                        part_own[c, d, i + k] = piece[at : at + part]
-                        part_send[c, d, i + k] = piece[mine + at : mine + at + part].astype(BF16)
+            for k, piece in enumerate(columns(left, d, ((high,), (low,)))):
+                for c in range(chains):
+                    at = c * part
+                    part_own[c, d, k] = piece[at : at + part]
+                    part_send[c, d, k] = piece[mine + at : mine + at + part].astype(BF16)
 
     def finish_start():
         for c in range(chains):
@@ -204,34 +181,29 @@
                 else:
                     own[c] = value
 
+    def turn(pairs, at):
+        @pl.loop(0, high.shape[0], unroll=4)
+        def _(b):
+            for source, target in pairs:
+                target[b, :, at : at + rows] = source[b].T
+
     def partials(c):
         left = jnp.concatenate([dual[0, chain(c), :], dual[1, chain(c), :]], axis=1)
         left = left.astype(BF16)
         for d in far_first + [0]:
-            blocks = owned(d)
-            for i in range(0, 4, 2):
-                value = columns(left, blocks[i : i + 2], both)
-                for k in range(2):
-                    piece = value[:, k * size : (k + 1) * size]
-                    if d:
-                        send1[c, d, i + k] = piece.astype(BF16)
-                    else:
-                        own[c, i + k] = piece
+            for k, piece in enumerate(columns(left, d, ((high, far_high), (low, far_low)))):
+                if d:
+                    send1[c, d, k] = piece.astype(BF16)
+                else:
+                    own[c, k] = piece
             if d:
                 reduce(c, d).start()
 
-    def merge(c, step):
+    def update(c):
         total = own[c]
         for d in near_first:
             reduce(c, d).wait_recv()
             total += recv1[c, d].astype(F32)
-        half[c] = total
-        send2[c, lax.rem(step, 2)] = total.astype(BF16)
-        cross(c, step).start()
-
-    def update(c, step):
-        cross(c, step).wait_recv()
-        total = half[c] + recv2[c, lax.rem(step, 2)].astype(F32)
         before = state[:, chain(c), :]
         cost = state[:, pl.ds(mine + c * part, part), :]
         upper_here = state[:, pl.ds(2 * mine, 1), :]
@@ -242,18 +214,17 @@
         state[:, chain(c), :] = updated
         for d in near_first:
             reduce(c, d).wait_send()
-        cross(c, step).wait_send()
 
     def image(c):
         total = None
         for d in [0] + near_first:
             if d:
                 gather(c, d).wait_recv()
-            blocks = owned(d)
-            left = jnp.concatenate([spread[c, d, i] for i in range(4)], axis=1)
-            for refs in both:
-                right = jnp.concatenate([side_by_side(ref, blocks) for ref in refs], axis=0)
-                value = dot(left, right, 1)
+            q = 2 * chip_at(d)
+            left = jnp.concatenate([spread[c, d, k] for k in range(2)], axis=1)
+            for ref in (high_turned, low_turned):
+                right = jnp.concatenate([ref[q], ref[q + 1]], axis=0)
+                value = dot(left, right)
                 total = value if total is None else total + value
         for k in range(2):
             dual[k, chain(c), :] = jnp.maximum(
@@ -265,7 +236,7 @@
             gather(c, d).wait_send()
 
     barrier = pltpu.get_barrier_semaphore()
-    others = [partner, mirror + core, mirror + 1 - core] + [peer(d) for d in near_first]
+    others = [partner] + [peer(d) for d in near_first]
     for other in others:
         pl.semaphore_signal(
             barrier, inc=1, device_id={"row": other}, device_id_type=pl.DeviceIdType.MESH
@@ -283,6 +254,10 @@
     load(3).wait()
     sum_tiles(tiles, order, summed, high, low)
     start()
+    pl.semaphore_wait(barrier, len(others))
+    for c in range(chains):
+        for d in far_first + [0]:
+            first_partial(c, d).start()
     for k in range(4, 8):
         load(k).wait()
     for source, offset in ((primal_start, 0), (objective, mine)):
@@ -292,35 +267,29 @@
     for h in range(2):
         packed[h, pl.ds(2 * mine, 8), :] = jnp.broadcast_to(upper[...], (8, size))
     bounds[...] = row_bound[...].T
-    pl.semaphore_wait(barrier, len(others))
-    for c in range(chains):
-        for d in far_first + [0]:
-            first_partial(c, d).start()
-    for k in (1, 2, 0):
-        start_state(k).start()
+    finish_start()
+    start_state().start()
     for k in range(2):
         rows_over(k).start()
     for k in range(2):
         matrix(k).start()
-    state[slot + core] = packed[core]
+    state[core] = packed[core]
     dual[0] = flipped[whole(core), :]
     bound[0] = bounds[whole(core), :]
-    finish_start()
-    for c in range(chains):
-        merge(c, 0)
-    for k in range(3):
-        start_state(k).wait()
+    turn(((high, high_turned), (low, low_turned)), 0)
+    start_state().wait()
     for k in range(2):
         rows_over(k).wait()
         matrix(k).wait()
+    turn(((far_high, high_turned), (far_low, low_turned)), rows)
     for c in range(chains):
-        for d in range(group):
+        for d in range(chips):
             first_partial(c, d).wait_send()
 
     def iteration(step, carry):
         more = step < ITERS - 1
         for c in range(chains):
-            update(c, step)
+            update(c)
 
             @pl.when(jnp.logical_not(more))
             def _():
@@ -334,16 +303,11 @@
             def _():
                 dual_back(c).start()
 
-        @pl.when(more)
-        def _():
-            for c in range(chains):
-                merge(c, step + 1)
-
         return carry
 
     lax.fori_loop(0, ITERS, iteration, 0)
     for c in range(chains):
-        primal_end[place(c), :] = state[slot + core, chain(c), :]
+        primal_end[place(c), :] = state[core, chain(c), :]
         dual_end[place(c), :] = dual[0, chain(c), :]
     for c in range(chains):
         primal_back(c).wait()
@@ -357,8 +321,8 @@
     size = tile_values.shape[1]
     count = primal_start.shape[1]
     blocks = n * primal_start.shape[0] // size
-    group = n // 4
-    assert blocks == n and n % 4 == 0 and group & (group - 1) == 0
+    chips = n // 2
+    assert blocks == n and n % 2 == 0 and chips & (chips - 1) == 0
     rows = dual_start.shape[0]
     row_blocks = rows // size
     tiles = tile_values.shape[0]
@@ -371,17 +335,13 @@
     matrix = pltpu.VMEM((blocks, rows, size), BF16)
     column = pltpu.VMEM(primal_start.shape, F32)
     row = pltpu.VMEM(dual_start.shape, F32)
-    pieces = pltpu.VMEM((chains, group, 4, part, size), BF16)
-    sums = pltpu.VMEM((chains, 4, part, size), F32)
-    turns = pltpu.VMEM((chains, 2, 4, part, size), BF16)
-    room = (
-        8 * blocks * rows * size + 6 * (tiles + 1) * size * size
-        + 32 * blocks * mine * size + (8 << 20)
-    )
+    row_flipped = pltpu.VMEM((count, rows), F32)
+    turned = pltpu.VMEM((blocks, size, 2 * rows), BF16)
+    pieces = pltpu.VMEM((chains, chips, 2, part, size), BF16)
     primal_end, dual_end = pl.pallas_call(
         functools.partial(iterate_kernel, n, chains),
         out_shape=(
-            jax.ShapeDtypeStruct((count, size), F32), jax.ShapeDtypeStruct((count, rows), F32)
+            pltpu.VMEM((count, size), F32), pltpu.VMEM((count, rows), F32)
         ),
         in_specs=[pl.BlockSpec(memory_space=pltpu.HBM)] * 8,
         out_specs=(vmem, vmem),
@@ -391,19 +351,18 @@
             column, column, pltpu.VMEM((1, size), F32), row, row,
             pltpu.VMEM((8, lanes), jnp.int32), pltpu.SMEM((8, lanes), jnp.int32),
             pltpu.VMEM((tiles + 1, size, size), F32),
-            matrix, matrix, matrix, matrix,
-            pltpu.VMEM((count, rows), F32), pltpu.VMEM((count, rows), F32),
-            pltpu.VMEM((2, count + 8, size), F32), pltpu.VMEM((4, count + 8, size), F32),
+            matrix, matrix, matrix, matrix, turned, turned,
+            row_flipped, row_flipped,
+            pltpu.VMEM((2, count + 8, size), F32), pltpu.VMEM((2, count + 8, size), F32),
             pltpu.VMEM((2, mine, rows), F32), pltpu.VMEM((2, mine, rows), F32),
-            pltpu.VMEM((chains, group, 4, part, size), F32), pieces, pieces,
-            sums, pieces, pieces, sums, turns, turns, pieces,
+            pltpu.VMEM((chains, chips, 2, part, size), F32), pieces, pieces,
+            pltpu.VMEM((chains, 2, part, size), F32), pieces, pieces, pieces,
             dma((8,)), dma(()),
         ]
-        + [dma((chains, group))] * 2 + [dma((2,))] * 4 + [dma((3,))] * 2
-        + [dma((chains, group))] * 2 + [dma((chains, 2))] * 2 + [dma((chains, group))] * 2
-        + [dma((2, chains))] * 2,
+        + [dma((chains, chips))] * 2 + [dma((2,))] * 4 + [dma(())] * 2
+        + [dma((chains, chips))] * 4 + [dma((2, chains))] * 2,
         compiler_params=pltpu.CompilerParams(
-            collective_id=0, has_side_effects=True, vmem_limit_bytes=room
+            collective_id=0, has_side_effects=True, vmem_limit_bytes=66000000
         ),
     )(
         tile_values, tile_row.reshape(1, -1), tile_col.reshape(1, -1), primal_start, objective,
@@ -417,6 +376,7 @@
         ),
         in_specs=[vmem] * 2,
         out_specs=(vmem, vmem),
+        compiler_params=pltpu.CompilerParams(vmem_limit_bytes=1 << 20),
     )(primal_end, dual_end)
 
 

time: 60.6 us -> 49.4 us (0.82)
  local copies, waits for them, and re-layouts: 8.3 us -> 0 us
  Pallas kernels: 51.3 us -> 48.6 us
    unnamed x20 -> x0, local copies, waits for them, and re-layouts: 8.3 us -> none
    pallas_call x1, Pallas kernels: 49.5 us -> 47.8 us  [body(): pl.pallas_call(functools.partial(iterate_kernel, n, chains), out_shape=(p...]
    pallas_call x1, Pallas kernels: 1.73 us -> 0.79 us  [body(): pl.pallas_call(finish_kernel, out_shape=(jax.ShapeDtypeStruct(primal_star...]
where the time goes in v3:
time: 49.4 us; the launch traced here: 49.2 us
  Pallas kernels  48.6 us (98%)
  between operations  0.64 us (1%)
    pallas_call x1, Pallas kernels, body(): pl.pallas_call(functools.partial(iterate_kernel, n, chains), out_shape=(p...  47.8 us

profile of v3, /device:TPU:0, one launch (start us, length us, event | category | flops | bytes accessed | tf_op | source)
XLA Modules:
  0.0 49.2 jit_solution(4075957087884488877)
XLA Ops:
  0.6 47.8 %shard_map.95 = (f32[128,128]{1,0:T(8,128)S(1)}, f32[128,256]{1,0:T(8,128)S(1)}) custom-call(bf16[64,128,128]{2,1,0:T(8,128)(2,1)} %tiles_in.1, s32[1,64]{1,0:T(1,128)} %bitcast.3, s32[1,64]{1,0:T(1,128)} %bitcast.4, f32[128,128]{1,0:T(8,128)} %primal_in.1, f32[128,128]{1,0:T(8,128)} %objective_in.1, f32[1,128]{1,0:T(1,128)} %bitcast.5, f32[256,128]{1,0:T(8,128)} %dual_in.1, ...), custom_call_target="tpu_custom_call" | custom-call | tf_op jit(solution)/shard_map/pallas_call | solution.py:341
  48.4 0.8 %shard_map.96 = (f32[128,128]{1,0:T(8,128)}, f32[256,128]{1,0:T(8,128)}) custom-call(f32[128,128]{1,0:T(8,128)S(1)} %get-tuple-element.4.primal, f32[128,256]{1,0:T(8,128)S(1)} %get-tuple-element.5.dual), custom_call_target="tpu_custom_call" | custom-call | tf_op jit(solution)/shard_map/pallas_call | solution.py:371

commit v4 on v3

--- a/solution.py
+++ b/solution.py
@@ -141,7 +141,7 @@
             dual.at[1, chain(c)], dual_end.at[place(c)], se.at[1, c], re.at[1, c], partner
         )
 
-    far_first = list(range(chips - 1, 0, -1))
+    far_first = [*range(chips - 1, 1, -2), *range(chips - 2, 0, -2), 1]
     near_first = list(range(1, chips))
 
     def dot(left, right):
@@ -169,6 +169,8 @@
                     at = c * part
                     part_own[c, d, k] = piece[at : at + part]
                     part_send[c, d, k] = piece[mine + at : mine + at + part].astype(BF16)
+            for c in range(chains):
+                first_partial(c, d).start()
 
     def finish_start():
         for c in range(chains):
@@ -253,11 +255,8 @@
     to_scalars.wait()
     load(3).wait()
     sum_tiles(tiles, order, summed, high, low)
+    pl.semaphore_wait(barrier, len(others))
     start()
-    pl.semaphore_wait(barrier, len(others))
-    for c in range(chains):
-        for d in far_first + [0]:
-            first_partial(c, d).start()
     for k in range(4, 8):
         load(k).wait()
     for source, offset in ((primal_start, 0), (objective, mine)):

time: 49.4 us -> 48.5 us (0.982)
  Pallas kernels: 48.6 us -> 47.7 us
    pallas_call x1, Pallas kernels: 47.8 us -> 46.9 us  [body(): pl.pallas_call(functools.partial(iterate_kernel, n, chains), out_shape=(p...]
where the time goes in v4:
time: 48.5 us; the launch traced here: 48.3 us
  Pallas kernels  47.7 us (98%)
  between operations  0.64 us (1%)
    pallas_call x1, Pallas kernels, body(): pl.pallas_call(functools.partial(iterate_kernel, n, chains), out_shape=(p...  46.9 us

profile of v4, /device:TPU:0, one launch (start us, length us, event | category | flops | bytes accessed | tf_op | source)
XLA Modules:
  0.0 48.3 jit_solution(2343397358987485645)
XLA Ops:
  0.6 46.9 %shard_map.95 = (f32[128,128]{1,0:T(8,128)S(1)}, f32[128,256]{1,0:T(8,128)S(1)}) custom-call(bf16[64,128,128]{2,1,0:T(8,128)(2,1)} %tiles_in.1, s32[1,64]{1,0:T(1,128)} %bitcast.3, s32[1,64]{1,0:T(1,128)} %bitcast.4, f32[128,128]{1,0:T(8,128)} %primal_in.1, f32[128,128]{1,0:T(8,128)} %objective_in.1, f32[1,128]{1,0:T(1,128)} %bitcast.5, f32[256,128]{1,0:T(8,128)} %dual_in.1, ...), custom_call_target="tpu_custom_call" | custom-call | tf_op jit(solution)/shard_map/pallas_call | solution.py:340
  47.6 0.8 %shard_map.96 = (f32[128,128]{1,0:T(8,128)}, f32[256,128]{1,0:T(8,128)}) custom-call(f32[128,128]{1,0:T(8,128)S(1)} %get-tuple-element.4.primal, f32[128,256]{1,0:T(8,128)S(1)} %get-tuple-element.5.dual), custom_call_target="tpu_custom_call" | custom-call | tf_op jit(solution)/shard_map/pallas_call | solution.py:370

commit v5 on v3

--- a/solution.py
+++ b/solution.py
@@ -9,6 +9,7 @@
 
 ITERS = 3
 CHAINS = 2
+PIECES = 1
 STEP = 0.4
 F32 = jnp.float32
 BF16 = jnp.bfloat16
@@ -19,46 +20,59 @@
     dual_out[...] = dual[...].T
 
 
-def order_tiles(tile_row, tile_col, table, row_blocks):
-    tiles = tile_row.shape[1]
+def order_tiles(tile_row, tile_col, table, row_blocks, pieces):
+    count = tile_row.shape[1]
+    tiles = count // pieces
     lanes = table.shape[1]
-    across = tile_col[...] * row_blocks + tile_row[...]
-    s = lax.broadcasted_iota(jnp.int32, (tiles, tiles), 0)
-    t = lax.broadcasted_iota(jnp.int32, (tiles, tiles), 1)
-    across = jnp.broadcast_to(across, (tiles, tiles))
-    down = jnp.sum(jnp.where(s == t, across, 0), axis=1, keepdims=True)
-    before = jnp.logical_or(across < down, jnp.logical_and(across == down, t < s))
-    rank = jnp.sum(before.astype(jnp.int32), axis=1, keepdims=True)
+    across = jnp.broadcast_to(tile_col[...] * row_blocks + tile_row[...], (tiles, count))
+    s = lax.broadcasted_iota(jnp.int32, (tiles, count), 0)
+    t = lax.broadcasted_iota(jnp.int32, (tiles, count), 1)
     lane = lax.broadcasted_iota(jnp.int32, (tiles, lanes), 1)
     index = lax.broadcasted_iota(jnp.int32, (tiles, lanes), 0)
-    here = rank == lane
-    table[0:1, :] = jnp.sum(jnp.where(here, index, 0), axis=0, keepdims=True)
-    table[1:2, :] = jnp.sum(jnp.where(here, down, 0), axis=0, keepdims=True)
-    below = jnp.sum((down <= lane).astype(jnp.int32), axis=0, keepdims=True)
-    equal = jnp.sum((down == lane).astype(jnp.int32), axis=0, keepdims=True)
-    table[2:3, :] = jnp.where(equal > 0, below - 1, tiles)
-
-
-def sum_tiles(tiles, order, sums, high, low):
-    count, size, _ = tiles.shape
+    for p in range(pieces):
+        here = t - p * tiles
+        down = jnp.sum(jnp.where(s == here, across, 0), axis=1, keepdims=True)
+        before = jnp.logical_or(across < down, jnp.logical_and(across == down, here < s))
+        before = jnp.logical_and(before, jnp.logical_and(here >= 0, here < tiles))
+        rank = jnp.sum(before.astype(jnp.int32), axis=1, keepdims=True)
+        placed = rank == lane
+        below = jnp.sum((down <= lane).astype(jnp.int32), axis=0, keepdims=True)
+        equal = jnp.sum((down == lane).astype(jnp.int32), axis=0, keepdims=True)
+        ordered = jnp.sum(jnp.where(placed, index, 0), axis=0, keepdims=True)
+        places = jnp.sum(jnp.where(placed, down, 0), axis=0, keepdims=True)
+        table[3 * p : 3 * p + 1, :] = ordered + p * tiles
+        table[3 * p + 1 : 3 * p + 2, :] = places
+        table[3 * p + 2 : 3 * p + 3, :] = (
+            jnp.where(equal > 0, below - 1, tiles) + p * (tiles + 1)
+        )
+
+
+def sum_tiles(tiles, order, sums, p, pieces):
+    size = tiles.shape[1]
+    count = tiles.shape[0] // pieces
+    first = p * (count + 1)
+    sums[first + count] = jnp.zeros((size, size), F32)
+
+    def add(r, total):
+        again = order[3 * p + 1, r] == order[3 * p + 1, jnp.maximum(r - 1, 0)]
+        total = jnp.where(again, total, 0.0) + tiles[order[3 * p, r]].astype(F32)
+        sums[first + r] = total
+        return total
+
+    lax.fori_loop(0, count, add, jnp.zeros((size, size), F32), unroll=4)
+
+
+def dense_column(order, sums, high, low, c, pieces):
+    size = sums.shape[1]
     row_blocks = high.shape[1] // size
-    sums[count] = jnp.zeros((size, size), F32)
-
-    def add(r, total):
-        again = order[1, r] == order[1, jnp.maximum(r - 1, 0)]
-        total = jnp.where(again, total, 0.0) + tiles[order[0, r]].astype(F32)
-        sums[r] = total
-        return total
-
-    lax.fori_loop(0, count, add, jnp.zeros((size, size), F32), unroll=4)
-
-    @pl.loop(0, high.shape[0], unroll=2)
-    def _(c):
-        for k in range(row_blocks):
-            value = sums[order[2, c * row_blocks + k]]
-            rounded = value.astype(BF16)
-            high[c, k * size : (k + 1) * size] = rounded
-            low[c, k * size : (k + 1) * size] = (value - rounded.astype(F32)).astype(BF16)
+    for k in range(row_blocks):
+        value = None
+        for p in range(pieces):
+            piece = sums[order[3 * p + 2, c * row_blocks + k]]
+            value = piece if value is None else value + piece
+        rounded = value.astype(BF16)
+        high[c, k * size : (k + 1) * size] = rounded
+        low[c, k * size : (k + 1) * size] = (value - rounded.astype(F32)).astype(BF16)
 
 
 def iterate_kernel(
@@ -104,10 +118,14 @@
     def load(k):
         src, dst = (
             (tile_col_in, tile_col), (tile_row_in, tile_row), (dual_in, dual_start),
-            (tiles_in, tiles), (primal_in, primal_start), (objective_in, objective),
-            (upper_in, upper), (bound_in, row_bound),
+            (primal_in, primal_start), (objective_in, objective), (upper_in, upper),
+            (bound_in, row_bound),
         )[k]
         return pltpu.make_async_copy(src, dst, sl.at[k])
+
+    def load_tiles(p):
+        here = pl.ds(p * (tiles.shape[0] // PIECES), tiles.shape[0] // PIECES)
+        return pltpu.make_async_copy(tiles_in.at[here], tiles.at[here], st.at[1 + p])
 
     def first_partial(c, d):
         return send(
@@ -141,8 +159,12 @@
             dual.at[1, chain(c)], dual_end.at[place(c)], se.at[1, c], re.at[1, c], partner
         )
 
-    far_first = list(range(chips - 1, 0, -1))
+    far_first = [*range(chips - 1, 1, -2), *range(chips - 2, 0, -2), 1]
     near_first = list(range(1, chips))
+    arrival = [
+        d for low, top in ((1, chips // 2), (chips // 2, chips)) for odd in (1, 0)
+        for d in range(top - 1, low - 1, -1) if d % 2 == odd
+    ]
 
     def dot(left, right):
         return lax.dot_general(
@@ -164,12 +186,13 @@
         left = jnp.concatenate([flipped[whole(core), :], flipped[whole(1 - core), :]], axis=0)
         left = left.astype(BF16)
         for d in far_first + [0]:
+            for k in range(2):
+                dense_column(order, summed, high, low, 2 * chip_at(d) + k, PIECES)
             for k, piece in enumerate(columns(left, d, ((high,), (low,)))):
                 for c in range(chains):
                     at = c * part
                     part_own[c, d, k] = piece[at : at + part]
                     part_send[c, d, k] = piece[mine + at : mine + at + part].astype(BF16)
-
     def finish_start():
         for c in range(chains):
             for d in far_first + [0]:
@@ -217,7 +240,7 @@
 
     def image(c):
         total = None
-        for d in [0] + near_first:
+        for d in [0] + arrival:
             if d:
                 gather(c, d).wait_recv()
             q = 2 * chip_at(d)
@@ -241,24 +264,31 @@
         pl.semaphore_signal(
             barrier, inc=1, device_id={"row": other}, device_id_type=pl.DeviceIdType.MESH
         )
-    for k in range(8):
-        load(k).start()
+    load(0).start()
+    load(1).start()
+    for p in range(PIECES):
+        load_tiles(p).start()
+    load(2).start()
     load(0).wait()
     load(1).wait()
-    order_tiles(tile_row, tile_col, table, rows // size)
-    to_scalars = pltpu.make_async_copy(table, order, st)
+    order_tiles(tile_row, tile_col, table, rows // size, PIECES)
+    to_scalars = pltpu.make_async_copy(table, order, st.at[0])
     to_scalars.start()
+    to_scalars.wait()
+    for p in range(PIECES):
+        load_tiles(p).wait()
+        sum_tiles(tiles, order, summed, p, PIECES)
+    for k in range(3, 7):
+        load(k).start()
     load(2).wait()
     flipped[...] = dual_start[...].T
-    to_scalars.wait()
-    load(3).wait()
-    sum_tiles(tiles, order, summed, high, low)
     start()
     pl.semaphore_wait(barrier, len(others))
     for c in range(chains):
         for d in far_first + [0]:
             first_partial(c, d).start()
-    for k in range(4, 8):
+    finish_start()
+    for k in range(3, 7):
         load(k).wait()
     for source, offset in ((primal_start, 0), (objective, mine)):
         value = source[...].T
@@ -267,7 +297,6 @@
     for h in range(2):
         packed[h, pl.ds(2 * mine, 8), :] = jnp.broadcast_to(upper[...], (8, size))
     bounds[...] = row_bound[...].T
-    finish_start()
     start_state().start()
     for k in range(2):
         rows_over(k).start()
@@ -278,13 +307,15 @@
     bound[0] = bounds[whole(core), :]
     turn(((high, high_turned), (low, low_turned)), 0)
     start_state().wait()
-    for k in range(2):
-        rows_over(k).wait()
-        matrix(k).wait()
-    turn(((far_high, high_turned), (far_low, low_turned)), rows)
-    for c in range(chains):
-        for d in range(chips):
-            first_partial(c, d).wait_send()
+
+    def finish_matrix():
+        for k in range(2):
+            rows_over(k).wait()
+            matrix(k).wait()
+        turn(((far_high, high_turned), (far_low, low_turned)), rows)
+        for c in range(chains):
+            for d in range(chips):
+                first_partial(c, d).wait_send()
 
     def iteration(step, carry):
         more = step < ITERS - 1
@@ -295,6 +326,7 @@
             def _():
                 primal_back(c).start()
 
+        pl.when(step == 0)(finish_matrix)
         for c in range(chains):
             image(c)
             pl.when(more)(functools.partial(partials, c))
@@ -330,6 +362,8 @@
     mine = count // 2
     part = mine // chains
     lanes = -(-max(tiles, blocks * row_blocks) // 128) * 128
+    table_rows = -(-3 * PIECES // 8) * 8
+    table = pltpu.VMEM((table_rows, lanes), jnp.int32)
     vmem = pl.BlockSpec(memory_space=pltpu.VMEM)
     dma = pltpu.SemaphoreType.DMA
     matrix = pltpu.VMEM((blocks, rows, size), BF16)
@@ -349,15 +383,15 @@
             pltpu.VMEM(tile_values.shape, BF16),
             pltpu.VMEM((1, tiles), jnp.int32), pltpu.VMEM((1, tiles), jnp.int32),
             column, column, pltpu.VMEM((1, size), F32), row, row,
-            pltpu.VMEM((8, lanes), jnp.int32), pltpu.SMEM((8, lanes), jnp.int32),
-            pltpu.VMEM((tiles + 1, size, size), F32),
+            table, pltpu.SMEM((table_rows, lanes), jnp.int32),
+            pltpu.VMEM((tiles + PIECES, size, size), F32),
             matrix, matrix, matrix, matrix, turned, turned,
             row_flipped, row_flipped,
             pltpu.VMEM((2, count + 8, size), F32), pltpu.VMEM((2, count + 8, size), F32),
             pltpu.VMEM((2, mine, rows), F32), pltpu.VMEM((2, mine, rows), F32),
             pltpu.VMEM((chains, chips, 2, part, size), F32), pieces, pieces,
             pltpu.VMEM((chains, 2, part, size), F32), pieces, pieces, pieces,
-            dma((8,)), dma(()),
+            dma((7,)), dma((1 + PIECES,)),
         ]
         + [dma((chains, chips))] * 2 + [dma((2,))] * 4 + [dma(())] * 2
         + [dma((chains, chips))] * 4 + [dma((2, chains))] * 2,

time: 49.4 us -> 47.5 us (0.962)
  Pallas kernels: 48.6 us -> 46.7 us
    pallas_call x1, Pallas kernels: 47.8 us -> 45.9 us  [body(): pl.pallas_call(functools.partial(iterate_kernel, n, chains), out_shape=(p...]
where the time goes in v5:
time: 47.5 us; the launch traced here: 47.3 us
  Pallas kernels  46.7 us (98%)
  between operations  0.64 us (1%)
    pallas_call x1, Pallas kernels, body(): pl.pallas_call(functools.partial(iterate_kernel, n, chains), out_shape=(p...  45.9 us

profile of v5, /device:TPU:0, one launch (start us, length us, event | category | flops | bytes accessed | tf_op | source)
XLA Modules:
  0.0 47.3 jit_solution(9898153796861696371)
XLA Ops:
  0.6 45.9 %shard_map.95 = (f32[128,128]{1,0:T(8,128)S(1)}, f32[128,256]{1,0:T(8,128)S(1)}) custom-call(bf16[64,128,128]{2,1,0:T(8,128)(2,1)} %tiles_in.1, s32[1,64]{1,0:T(1,128)} %bitcast.3, s32[1,64]{1,0:T(1,128)} %bitcast.4, f32[128,128]{1,0:T(8,128)} %primal_in.1, f32[128,128]{1,0:T(8,128)} %objective_in.1, f32[1,128]{1,0:T(1,128)} %bitcast.5, f32[256,128]{1,0:T(8,128)} %dual_in.1, ...), custom_call_target="tpu_custom_call" | custom-call | tf_op jit(solution)/shard_map/pallas_call | solution.py:375
  46.5 0.8 %shard_map.96 = (f32[128,128]{1,0:T(8,128)}, f32[256,128]{1,0:T(8,128)}) custom-call(f32[128,128]{1,0:T(8,128)S(1)} %get-tuple-element.4.primal, f32[128,256]{1,0:T(8,128)S(1)} %get-tuple-element.5.dual), custom_call_target="tpu_custom_call" | custom-call | tf_op jit(solution)/shard_map/pallas_call | solution.py:405

commit v6 on v5

--- a/solution.py
+++ b/solution.py
@@ -15,9 +15,21 @@
 BF16 = jnp.bfloat16
 
 
-def finish_kernel(primal, dual, primal_out, dual_out):
-    primal_out[...] = primal[...].T
-    dual_out[...] = dual[...].T
+def finish_kernel(primal, dual, primal_out, dual_out, primal_turned, dual_turned, sems):
+    size = primal.shape[1]
+    copies = []
+    for k in range(dual.shape[1] // size):
+        here = pl.ds(k * size, size)
+        dual_turned[here, :] = dual[:, here].T
+        copies.append(
+            pltpu.make_async_copy(dual_turned.at[here], dual_out.at[here], sems.at[k + 1])
+        )
+        copies[-1].start()
+    primal_turned[...] = primal[...].T
+    copies.append(pltpu.make_async_copy(primal_turned, primal_out, sems.at[0]))
+    copies[-1].start()
+    for copy in copies:
+        copy.wait()
 
 
 def order_tiles(tile_row, tile_col, table, row_blocks, pieces):
@@ -317,27 +329,22 @@
             for d in range(chips):
                 first_partial(c, d).wait_send()
 
-    def iteration(step, carry):
+    def iteration(step):
         more = step < ITERS - 1
         for c in range(chains):
             update(c)
-
-            @pl.when(jnp.logical_not(more))
-            def _():
+            if not more:
                 primal_back(c).start()
-
-        pl.when(step == 0)(finish_matrix)
+        if step == 0:
+            finish_matrix()
         for c in range(chains):
             image(c)
-            pl.when(more)(functools.partial(partials, c))
-
-            @pl.when(jnp.logical_not(more))
-            def _():
+            if more:
+                partials(c)
+            else:
                 dual_back(c).start()
-
-        return carry
-
-    lax.fori_loop(0, ITERS, iteration, 0)
+    for step in range(ITERS):
+        iteration(step)
     for c in range(chains):
         primal_end[place(c), :] = state[core, chain(c), :]
         dual_end[place(c), :] = dual[0, chain(c), :]
@@ -409,7 +416,8 @@
             jax.ShapeDtypeStruct(dual_start.shape, F32),
         ),
         in_specs=[vmem] * 2,
-        out_specs=(vmem, vmem),
+        out_specs=(pl.BlockSpec(memory_space=pltpu.HBM),) * 2,
+        scratch_shapes=[column, row, dma((1 + row_blocks,))],
         compiler_params=pltpu.CompilerParams(vmem_limit_bytes=1 << 20),
     )(primal_end, dual_end)
 

time: 47.5 us -> 47.2 us (level)
  no operation moved by 1% of the time
where the time goes in v6:
time: 47.2 us; the launch traced here: 47.1 us
  Pallas kernels  46.4 us (98%)
  between operations  0.64 us (1%)
    pallas_call x1, Pallas kernels, body(): pl.pallas_call(functools.partial(iterate_kernel, n, chains), out_shape=(p...  45.6 us

profile of v6, /device:TPU:0, one launch (start us, length us, event | category | flops | bytes accessed | tf_op | source)
XLA Modules:
  0.0 47.1 jit_solution(8817743207982622084)
XLA Ops:
  0.6 45.6 %shard_map.95 = (f32[128,128]{1,0:T(8,128)S(1)}, f32[128,256]{1,0:T(8,128)S(1)}) custom-call(bf16[64,128,128]{2,1,0:T(8,128)(2,1)} %tiles_in.1, s32[1,64]{1,0:T(1,128)} %bitcast.3, s32[1,64]{1,0:T(1,128)} %bitcast.4, f32[128,128]{1,0:T(8,128)} %primal_in.1, f32[128,128]{1,0:T(8,128)} %objective_in.1, f32[1,128]{1,0:T(1,128)} %bitcast.5, f32[256,128]{1,0:T(8,128)} %dual_in.1, ...), custom_call_target="tpu_custom_call" | custom-call | tf_op jit(solution)/shard_map/pallas_call | solution.py:382
  46.3 0.8 %shard_map.96 = (f32[128,128]{1,0:T(8,128)}, f32[256,128]{1,0:T(8,128)}) custom-call(f32[128,128]{1,0:T(8,128)S(1)} %get-tuple-element.4.primal, f32[128,256]{1,0:T(8,128)S(1)} %get-tuple-element.5.dual), custom_call_target="tpu_custom_call" | custom-call | tf_op jit(solution)/shard_map/pallas_call | solution.py:412

commit v7 on v6

--- a/solution.py
+++ b/solution.py
@@ -217,7 +217,7 @@
                     own[c] = value
 
     def turn(pairs, at):
-        @pl.loop(0, high.shape[0], unroll=4)
+        @pl.loop(0, high.shape[0], unroll=8)
         def _(b):
             for source, target in pairs:
                 target[b, :, at : at + rows] = source[b].T
@@ -234,7 +234,7 @@
             if d:
                 reduce(c, d).start()
 
-    def update(c):
+    def update(c, more):
         total = own[c]
         for d in near_first:
             reduce(c, d).wait_recv()
@@ -244,11 +244,13 @@
         upper_here = state[:, pl.ds(2 * mine, 1), :]
         updated = jnp.clip(before - STEP * (cost - total), 0.0, upper_here)
         spread[c, 0] = (2.0 * updated - before).astype(BF16)
-        for d in far_first:
-            gather(c, d).start()
+        if more:
+            for d in far_first:
+                gather(c, d).start()
+        else:
+            for q in range(chips):
+                pl.when(chip != q)(gather(c, lax.bitwise_xor(chip, q)).start)
         state[:, chain(c), :] = updated
-        for d in near_first:
-            reduce(c, d).wait_send()
 
     def image(c):
         total = None
@@ -268,6 +270,7 @@
                 0.0,
             )
         for d in near_first:
+            reduce(c, d).wait_send()
             gather(c, d).wait_send()
 
     barrier = pltpu.get_barrier_semaphore()
@@ -332,7 +335,7 @@
     def iteration(step):
         more = step < ITERS - 1
         for c in range(chains):
-            update(c)
+            update(c, more)
             if not more:
                 primal_back(c).start()
         if step == 0:

time: 47.2 us -> 47.2 us (level)
  no operation moved by 1% of the time
where the time goes in v7:
time: 47.2 us; the launch traced here: 47 us
  Pallas kernels  46.4 us (98%)
  between operations  0.64 us (1%)
    pallas_call x1, Pallas kernels, body(): pl.pallas_call(functools.partial(iterate_kernel, n, chains), out_shape=(p...  45.6 us

profile of v7, /device:TPU:0, one launch (start us, length us, event | category | flops | bytes accessed | tf_op | source)
XLA Modules:
  0.0 47.0 jit_solution(3635609564652300964)
XLA Ops:
  0.6 45.6 %shard_map.95 = (f32[128,128]{1,0:T(8,128)S(1)}, f32[128,256]{1,0:T(8,128)S(1)}) custom-call(bf16[64,128,128]{2,1,0:T(8,128)(2,1)} %tiles_in.1, s32[1,64]{1,0:T(1,128)} %bitcast.3, s32[1,64]{1,0:T(1,128)} %bitcast.4, f32[128,128]{1,0:T(8,128)} %primal_in.1, f32[128,128]{1,0:T(8,128)} %objective_in.1, f32[1,128]{1,0:T(1,128)} %bitcast.5, f32[256,128]{1,0:T(8,128)} %dual_in.1, ...), custom_call_target="tpu_custom_call" | custom-call | tf_op jit(solution)/shard_map/pallas_call | solution.py:385
  46.2 0.8 %shard_map.96 = (f32[128,128]{1,0:T(8,128)}, f32[256,128]{1,0:T(8,128)}) custom-call(f32[128,128]{1,0:T(8,128)S(1)} %get-tuple-element.4.primal, f32[128,256]{1,0:T(8,128)S(1)} %get-tuple-element.5.dual), custom_call_target="tpu_custom_call" | custom-call | tf_op jit(solution)/shard_map/pallas_call | solution.py:415
